TPU v7x, 128 devices: a whole 4x4x4 slice. The times are simulated.
128 devices in a mesh: freq: 8 (over x, core), blk: 16 (over y, z).
Axes of the slice: x: 4, y: 4, z: 4, core: 2. Of those that a mesh axis runs over, the one named last changes fastest.
Arguments:
- sky_maps: bfloat16 [8, 256, 32, 8192], P('freq', 'blk'), may hold values from -24 to 24
- legendre: bfloat16 [128, 256, 4096], P('blk')
- mode_values: int32 [128], replicated, may hold values from 0 to 4095, as said below
- cycle_order: int32 [256], replicated, may hold values from 0 to 255, each once
- bin_widths: int32 [128], replicated, may hold values from 1 to 512, 4096 in all
Outputs:
- cleaned: float32 [32, 2, 128, 4096], P(None, None, None, ('freq', 'blk'))
Inputs may be any that keep to these rules, and one draw needn't show every extreme that they name: Distinct values, 0 and 4095 among them; legendre[s, q, l] is zero wherever l < mode_values[s]. `cycle_order`: each cycle index once.
All inputs are finite; a program needn't handle non-finite values.
Results may differ from a plain program's by a relative error of at most 0.0036.
Values may be sent and summed in bfloat16 or wider, within the bound.
A program may use at most 192 MiB of HBM per device.

v0:
```python
import math
import jax
import jax.numpy as jnp
from jax import lax
from jax.sharding import PartitionSpec as P


def build_trig(mode_values, pixel_count):
    pixels = jnp.arange(pixel_count, dtype=jnp.int32)
    phase_index = pixels[:, None] * mode_values[None, :] % pixel_count
    angles = phase_index.astype(jnp.float32) * jnp.float32(2.0 * math.pi / pixel_count)
    factor = jnp.float32(pixel_count ** (-0.5))
    return (jnp.cos(angles) * factor, -jnp.sin(angles) * factor)


def ilc_weights(spectra):
    chan_count = spectra.shape[1]
    trace_value = jnp.trace(spectra, axis1=1, axis2=2)
    identity = jnp.eye(chan_count, dtype=jnp.float32)
    loaded = (
        spectra
        + (jnp.float32(0.1) * trace_value / jnp.float32(chan_count))[:, None, None] * identity[None]
    )
    lower_factor = jnp.linalg.cholesky(loaded)
    unit_vector = jnp.ones(spectra.shape[:2] + (1,), jnp.float32)
    forward = jax.scipy.linalg.solve_triangular(lower_factor, unit_vector, lower=True)
    solved = jax.scipy.linalg.solve_triangular(lower_factor, forward, trans=1, lower=True)[..., 0]
    return solved / jnp.sum(solved, axis=1, keepdims=True)


def project_mode(left_side, table_rows):
    dims = (((0,), (0,)), ((), ()))
    return lax.dot_general(left_side, table_rows, dims, preferred_element_type=jnp.float32).astype(
        jnp.bfloat16
    )


def clean_band(pieces, ell_start, multiplier, bin_widths):
    chan_count = pieces.shape[0]
    ell_span = pieces.shape[4]
    weighted = pieces * multiplier.astype(jnp.bfloat16)[None, None, None, :, None]
    per_ell = jnp.einsum("ikcsl,jkcsl->ijl", weighted, pieces, preferred_element_type=jnp.float32)
    bin_ends = jnp.cumsum(bin_widths)
    begins = bin_ends - bin_widths
    ell_values = ell_start + jnp.arange(ell_span, dtype=jnp.int32)
    onehot = (
        (ell_values[:, None] >= begins[None, :]) & (ell_values[:, None] < bin_ends[None, :])
    ).astype(jnp.float32)
    partial_value = jnp.dot(
        per_ell.reshape(chan_count * chan_count, ell_span), onehot, precision=lax.Precision.HIGHEST
    )
    spectra = lax.psum(partial_value, ("freq", "blk"))
    weights = ilc_weights(spectra.T.reshape(bin_widths.shape[0], chan_count, chan_count))
    per_ell_weights = jnp.dot(onehot, weights, precision=lax.Precision.HIGHEST)
    return jnp.einsum(
        "ikcsl,li->kcsl",
        pieces.astype(jnp.float32),
        per_ell_weights,
        precision=lax.Precision.HIGHEST,
    )


def on_device(sky_maps, legendre, mode_values, cycle_order, bin_widths):
    groups = lax.axis_size("blk")
    per_device = legendre.shape[0]
    row_count = sky_maps.shape[1]
    map_count = sky_maps.shape[2]
    pixel_count = sky_maps.shape[3]
    ell_count = legendre.shape[2]
    cos_part, sin_part = build_trig(mode_values, pixel_count)
    fourier = jnp.stack(
        [
            cos_part.reshape(pixel_count, groups, per_device),
            sin_part.reshape(pixel_count, groups, per_device),
        ],
        axis=2,
    )
    fourier = fourier.reshape(pixel_count, groups * 2 * per_device).astype(jnp.bfloat16)
    fourier_rows = jnp.dot(
        sky_maps.reshape(row_count * map_count, pixel_count),
        fourier,
        preferred_element_type=jnp.float32,
    )
    fourier_rows = fourier_rows.astype(jnp.bfloat16).reshape(
        row_count, map_count, groups * 2 * per_device
    )
    inverse = jnp.argsort(cycle_order)
    block_index = lax.axis_index("blk")
    freq_index = lax.axis_index("freq")
    multiplier = jnp.where(mode_values > 0, 2.0, 1.0).astype(jnp.float32)
    gathered = lax.all_to_all(fourier_rows, "blk", split_axis=2, concat_axis=0, tiled=True)
    ordered = gathered[inverse]
    item_count = ordered.shape[1]
    results = []
    for slot_index in range(per_device):
        left_side = ordered[:, :, slot_index::per_device].reshape(ordered.shape[0], item_count * 2)
        results.append(project_mode(left_side, legendre[slot_index]))
    stacked = jnp.stack(results, axis=1)
    coeffs = stacked.reshape(item_count, 2, per_device, ell_count)
    pieces = lax.all_to_all(
        lax.all_to_all(coeffs[None], "freq", split_axis=4, concat_axis=0, tiled=True),
        "blk",
        split_axis=4,
        concat_axis=3,
        tiled=True,
    )
    ell_start = (freq_index * groups + block_index) * pieces.shape[4]
    cleaned = clean_band(pieces, ell_start, multiplier, bin_widths)
    return cleaned


def solution(mesh):
    return jax.shard_map(
        on_device,
        mesh=mesh,
        in_specs=(P("freq", "blk", None, None), P("blk", None, None), P(), P(), P()),
        out_specs=P(None, None, None, ("freq", "blk")),
        check_vma=False,
    )
```

profile of v0, /device:TPU:1, one launch (start us, length us, event | category | flops | bytes accessed | tf_op | source)
XLA Modules:
  0.0 697.8 jit_solution(2399682190589871519)
XLA Ops:
  0.7 18.3 %multiply_convert_fusion.1 = (bf16[8192,16,1,8]{0,3,2,1:T(8,128)(2,1)S(1)}, bf16[8192,16,1,8]{0,3,2,1:T(8,128)(2,1)S(1)}) fusion(s32[16,8]{1,0:T(8,128)S(1)} %mul.96), kind=kLoop, calls=%fused_computation.19 | loop fusion | flops 19922944 | bytes 4194816 | tf_op jit(solution)/shard_map/convert
  19.5 3.0 copy-done.3
  22.4 2.4 fusion.22
  25.9 1.7 reshape.236
  27.6 8.6 %all-to-all-start = ((bf16[16,2,4096]{2,1,0:T(2,128)(2,1)}), bf16[16,2,4096]{2,1,0:T(2,128)(2,1)S(1)}, u32[]{:S(2)}, u32[]{:S(2)}) async-start(bf16[16,2,4096]{2,1,0:T(2,128)(2,1)} %reshape.236), calls=%async_computation | async-start | bytes 524288 | tf_op jit(solution)/shard_map/all_to_all | solution.py:91
  36.2 3.2 sort.17
  39.4 4.2 all-to-all-done
  45.3 1.4 slice.66
  46.7 1.4 slice.68
  48.2 1.4 slice.70
  49.6 1.4 slice.72
  51.0 1.4 slice.74
  52.5 1.4 slice.76
  53.9 1.4 slice.78
  56.9 2.1 convolution_convert_fusion.7
  59.3 7.4 %copy.174 = bf16[1,32,2,1,4096]{1,3,2,0,4:T(2,128)(2,1)} copy(bf16[1,32,2,1,4096]{4,2,1,3,0:T(2,128)(2,1)S(1)} %stack.32) | data formatting | bytes 1048576 | tf_op jit(solution)/shard_map/stack | solution.py:98
  66.9 2.1 convolution_convert_fusion.6
  69.3 7.4 %copy.175 = bf16[1,32,2,1,4096]{1,3,2,0,4:T(2,128)(2,1)} copy(bf16[1,32,2,1,4096]{4,2,1,3,0:T(2,128)(2,1)S(1)} %stack.33) | data formatting | bytes 1048576 | tf_op jit(solution)/shard_map/stack | solution.py:98
  76.8 2.1 convolution_convert_fusion.5
  79.2 7.4 %copy.176 = bf16[1,32,2,1,4096]{1,3,2,0,4:T(2,128)(2,1)} copy(bf16[1,32,2,1,4096]{4,2,1,3,0:T(2,128)(2,1)S(1)} %stack.34) | data formatting | bytes 1048576 | tf_op jit(solution)/shard_map/stack | solution.py:98
  86.8 2.1 convolution_convert_fusion.4
  89.2 7.4 %copy.177 = bf16[1,32,2,1,4096]{1,3,2,0,4:T(2,128)(2,1)} copy(bf16[1,32,2,1,4096]{4,2,1,3,0:T(2,128)(2,1)S(1)} %stack.35) | data formatting | bytes 1048576 | tf_op jit(solution)/shard_map/stack | solution.py:98
  96.7 2.1 convolution_convert_fusion.3
  99.1 7.4 %copy.178 = bf16[1,32,2,1,4096]{1,3,2,0,4:T(2,128)(2,1)} copy(bf16[1,32,2,1,4096]{4,2,1,3,0:T(2,128)(2,1)S(1)} %stack.36) | data formatting | bytes 1048576 | tf_op jit(solution)/shard_map/stack | solution.py:98
  106.6 2.1 convolution_convert_fusion.2
  109.1 7.4 %copy.179 = bf16[1,32,2,1,4096]{1,3,2,0,4:T(2,128)(2,1)} copy(bf16[1,32,2,1,4096]{4,2,1,3,0:T(2,128)(2,1)S(1)} %stack.37) | data formatting | bytes 1048576 | tf_op jit(solution)/shard_map/stack | solution.py:98
  116.6 2.1 convolution_convert_fusion.1
  119.0 7.4 %copy.180 = bf16[1,32,2,1,4096]{1,3,2,0,4:T(2,128)(2,1)} copy(bf16[1,32,2,1,4096]{4,2,1,3,0:T(2,128)(2,1)S(1)} %stack.38) | data formatting | bytes 1048576 | tf_op jit(solution)/shard_map/stack | solution.py:98
  126.5 2.1 convolution_convert_fusion
  128.9 7.4 %copy.181 = bf16[1,32,2,1,4096]{1,3,2,0,4:T(2,128)(2,1)} copy(bf16[1,32,2,1,4096]{4,2,1,3,0:T(2,128)(2,1)S(1)} %stack.39) | data formatting | bytes 1048576 | tf_op jit(solution)/shard_map/stack | solution.py:98
  136.3 85.4 %stack.40 = bf16[1,32,2,8,4096]{1,3,2,0,4:T(8,128)(2,1)} concatenate(bf16[1,32,2,1,4096]{1,3,2,0,4:T(2,128)(2,1)} %copy.174, bf16[1,32,2,1,4096]{1,3,2,0,4:T(2,128)(2,1)} %copy.175, bf16[1,32,2,1,4096]{1,3,2,0,4:T(2,128)(2,1)} %copy.176, bf16[1,32,2,1,4096]{1,3,2,0,4:T(2,128)(2,1)} %copy.177, bf16[1,32,2,1,4096]{1,3,2,0,4:T(2,128)(2,1)} %copy.178, ...), dimensions={3} | concatenate | bytes 8388608 | tf_op jit(solution)/shard_map/stack | solution.py:98
  221.7 18.9 %reshape.238 = bf16[8,2,131072]{2,1,0:T(2,128)(2,1)} reshape(bf16[4096,1,2,8,32]{4,3,2,1,0:T(8,128)(2,1)} %bitcast.108) | data formatting | bytes 8388608
  240.6 55.1 %all_to_all.54 = bf16[8,2,131072]{2,1,0:T(2,128)(2,1)} all-to-all(bf16[8,2,131072]{2,1,0:T(2,128)(2,1)} %reshape.238), channel_id=1, replica_groups=mesh['freq'=8,'blk'=16] {'freq'}, dimensions={0} | all-to-all | bytes 8388608 | tf_op jit(solution)/shard_map/all_to_all | solution.py:101
  295.7 12.4 %reshape.239 = bf16[4096,1,2,8,32]{4,3,2,1,0:T(8,128)(2,1)} reshape(bf16[8,2,131072]{2,1,0:T(2,128)(2,1)} %all_to_all.54) | data formatting | bytes 8388608
  308.2 15.3 %copy.218 = bf16[8,32,2,8,512]{1,3,2,0,4:T(8,128)(2,1)} copy(bf16[8,32,2,8,512]{1,3,2,4,0:T(8,128)(2,1)} %bitcast.109) | data formatting | bytes 8388608 | tf_op jit(solution)/shard_map/all_to_all | solution.py:101
  323.5 20.8 %reshape.240 = bf16[16,2,65536]{2,1,0:T(2,128)(2,1)} reshape(bf16[512,8,2,8,32]{4,3,2,1,0:T(8,128)(2,1)} %bitcast.110) | data formatting | bytes 8388608
  344.2 4.7 all-to-all-start.2
  349.5 59.1 %all-to-all-done.2 = bf16[16,2,65536]{2,1,0:T(2,128)(2,1)} async-done(((bf16[16,2,65536]{2,1,0:T(2,128)(2,1)}), bf16[16,2,65536]{2,1,0:T(2,128)(2,1)}, u32[]{:S(2)}, u32[]{:S(2)}) %all-to-all-start.2) | async-done | bytes 4194336 | tf_op jit(solution)/shard_map/all_to_all | solution.py:100
  408.6 16.0 %reshape.241 = bf16[512,8,2,8,32]{4,3,2,1,0:T(8,128)(2,1)} reshape(bf16[16,2,65536]{2,1,0:T(2,128)(2,1)} %all-to-all-done.2) | data formatting | bytes 8388608
  424.6 36.1 %copy.185 = bf16[8,32,2,16,8,32]{5,4,3,2,1,0:T(8,128)(2,1)} copy(bf16[8,32,2,16,8,32]{1,4,2,0,5,3:T(8,128)(2,1)} %bitcast.111) | data formatting | bytes 8388608 | tf_op jit(solution)/shard_map/all_to_all | solution.py:100
  460.7 14.3 %broadcast_multiply_fusion = bf16[8,32,2,128,32]{4,3,2,1,0:T(8,128)(2,1)} fusion(bf16[128]{0:T(256)(128)(2,1)S(1)} %fusion.35, bf16[8,32,2,16,8,32]{5,4,3,2,1,0:T(8,128)(2,1)} %copy.185), kind=kLoop, calls=%fused_computation.2 | loop fusion | flops 2097152 | bytes 8388864 | tf_op jit(solution)/shard_map/mul | solution.py:41
  475.0 16.1 %copy.187 = bf16[8,32,2,128,32]{3,0,1,2,4:T(8,128)(2,1)} copy(bf16[8,32,2,128,32]{4,3,2,1,0:T(8,128)(2,1)} %broadcast_multiply_fusion) | data formatting | bytes 8388608 | tf_op jit(solution)/shard_map/mul | solution.py:41
  491.1 16.0 %copy.186 = bf16[8,32,2,128,32]{3,0,1,2,4:T(8,128)(2,1)} copy(bf16[8,32,2,128,32]{4,3,2,1,0:T(8,128)(2,1)} %bitcast.107) | data formatting | bytes 8388608 | tf_op jit(solution)/shard_map/all_to_all | solution.py:100
  507.1 6.3 convolution_bitcast_fusion
  513.7 70.2 %psum.7 = f32[128,64]{0,1:T(8,128)S(1)} all-reduce(f32[128,64]{0,1:T(8,128)S(1)} %fusion.23), channel_id=1, replica_groups=mesh['freq'=8,'blk'=16] {'freq','blk'}, use_global_device_ids=true, to_apply=%region_2.3 | all-reduce | flops 8192 | bytes 65536 | tf_op jit(solution)/shard_map/psum | solution.py:52
  584.4 93.9 %custom-call.11 = f32[128,8,8]{2,1,0:T(8,128)S(1)} custom-call(f32[128,8,8]{2,1,0:T(8,128)S(1)} %broadcast_multiply_fusion.1), custom_call_target="Cholesky" | custom-call | tf_op jit(solution)/shard_map/jit(cholesky)/cholesky | solution.py:24
  681.0 13.2 %multiply_reduce_fusion = f32[32,32,2,128]{0,3,2,1:T(8,128)} fusion(f32[32,8]{0,1:T(8,128)S(1)} %fusion.25, bf16[8,32,2,16,8,32]{5,4,3,2,1,0:T(8,128)(2,1)} %copy.185), kind=kLoop, calls=%fused_computation.1 | loop fusion | flops 6029312 | bytes 5243904
  694.2 3.6 copy.207
  (72 shorter events, 12.8 us)
Async XLA Ops:
  19.1 3.4 copy-start.3
  22.4 13.8 %copy-start = (s32[256]{0:T(256)S(1)}, s32[256]{0:T(256)}, u32[]{:S(2)}) copy-start(s32[256]{0:T(256)} %param.8) | copy-start | bytes 3076
  27.6 16.1 %all-to-all-start = ((bf16[16,2,4096]{2,1,0:T(2,128)(2,1)}), bf16[16,2,4096]{2,1,0:T(2,128)(2,1)S(1)}, u32[]{:S(2)}, u32[]{:S(2)}) async-start(bf16[16,2,4096]{2,1,0:T(2,128)(2,1)} %reshape.236), calls=%async_computation | async-start | bytes 524288 | tf_op jit(solution)/shard_map/all_to_all | solution.py:91
  344.2 4.7 copy-start.1
  344.2 5.2 copy-start.2
  344.2 64.3 %all-to-all-start.2 = ((bf16[16,2,65536]{2,1,0:T(2,128)(2,1)}), bf16[16,2,65536]{2,1,0:T(2,128)(2,1)}, u32[]{:S(2)}, u32[]{:S(2)}) async-start(bf16[16,2,65536]{2,1,0:T(2,128)(2,1)} %reshape.240), calls=%async_computation.2 | async-start | bytes 8388608 | tf_op jit(solution)/shard_map/all_to_all | solution.py:100
where the time goes:
time: 711 us; the launch traced here: 698 us
  local copies, waits for them, and re-layouts  324 us (46%)
  other arithmetic  145 us (20%)
  blocking collectives  125 us (18%)
  waiting for transfers between devices  63.3 us (9%)
  matrix products  26.6 us (4%)
  starting transfers between devices  13.3 us (2%)
    another operation x17, local copies, waits for them, and re-layouts, on_device(): stacked = jnp.stack(results, axis=1)  147 us
    another operation x4, other arithmetic, ilc_weights(): lower_factor = jnp.linalg.cholesky(loaded)  94.1 us
    unnamed x15, local copies, waits for them, and re-layouts  73.4 us
    psum x1, blocking collectives, clean_band(): spectra = lax.psum(partial_value, ('freq', 'blk'))  70.2 us
    all_to_all x1, waiting for transfers between devices, on_device(): lax.all_to_all(lax.all_to_all(coeffs[None], 'freq', split_axis=4, concat_...  59.1 us
    all_to_all x1, blocking collectives, on_device(): lax.all_to_all(coeffs[None], 'freq', split_axis=4, concat_axis=0, tiled=T...  55.1 us
    all_to_all x2, local copies, waits for them, and re-layouts, on_device(): lax.all_to_all(lax.all_to_all(coeffs[None], 'freq', split_axis=4, concat_...  52.1 us
    another operation x3, other arithmetic  18.6 us
  transfers between devices with their start and end apart: 2, of which 2 were waited for; matrix products, arithmetic and copies ran while one was open for 1% of the time, Pallas kernels for 0%

commit v1 on v0

--- a/solution.py
+++ b/solution.py
@@ -98,7 +98,12 @@
     stacked = jnp.stack(results, axis=1)
     coeffs = stacked.reshape(item_count, 2, per_device, ell_count)
     pieces = lax.all_to_all(
-        lax.all_to_all(coeffs[None], "freq", split_axis=4, concat_axis=0, tiled=True),
+        jnp.concatenate(
+            lax.all_to_all(
+                jnp.stack(jnp.split(coeffs[None], lax.axis_size("freq"), axis=4)), "freq", 0, 0
+            ),
+            axis=0,
+        ),
         "blk",
         split_axis=4,
         concat_axis=3,

time: 711 us -> 608 us (0.86)
  local copies, waits for them, and re-layouts: 324 us -> 223 us
    another operation x17 -> x9, local copies, waits for them, and re-layouts: 147 us -> 44 us  [on_device(): stacked = jnp.stack(results, axis=1)]
    reshape x0 -> x1, local copies, waits for them, and re-layouts: none -> 28.4 us  [on_device(): jnp.concatenate(lax.all_to_all(jnp.stack(jnp.split(coeffs[None], lax.axis...]
    unnamed x15 -> x20, local copies, waits for them, and re-layouts: 73.4 us -> 49.6 us
    all_to_all x3 -> x2, local copies, waits for them, and re-layouts: 67.4 us -> 52.1 us  [on_device(): lax.all_to_all(jnp.concatenate(lax.all_to_all(jnp.stack(jnp.split(coeffs[...]
    slice x16, local copies, waits for them, and re-layouts: 12.2 us -> 20.1 us  [on_device(): ordered[:, :, slot_index::per_device]]
where the time goes in v1:
time: 608 us; the launch traced here: 602 us
  local copies, waits for them, and re-layouts  223 us (37%)
  other arithmetic  145 us (24%)
  blocking collectives  122 us (20%)
  waiting for transfers between devices  66.9 us (11%)
  matrix products  31.4 us (5%)
  starting transfers between devices  13.5 us (2%)
    another operation x4, other arithmetic, ilc_weights(): lower_factor = jnp.linalg.cholesky(loaded)  94.1 us
    psum x1, blocking collectives, clean_band(): spectra = lax.psum(partial_value, ('freq', 'blk'))  67.2 us
    all_to_all x1, waiting for transfers between devices, on_device(): lax.all_to_all(jnp.concatenate(lax.all_to_all(jnp.stack(jnp.split(coeffs[...  62.7 us
    all_to_all x1, blocking collectives, on_device(): lax.all_to_all(jnp.stack(jnp.split(coeffs[None], lax.axis_size('freq'), a...  54.8 us
    all_to_all x2, local copies, waits for them, and re-layouts, on_device(): lax.all_to_all(jnp.concatenate(lax.all_to_all(jnp.stack(jnp.split(coeffs[...  52.1 us
    unnamed x20, local copies, waits for them, and re-layouts  49.6 us
    another operation x9, local copies, waits for them, and re-layouts, on_device(): stacked = jnp.stack(results, axis=1)  44 us
    reshape x1, local copies, waits for them, and re-layouts, on_device(): jnp.concatenate(lax.all_to_all(jnp.stack(jnp.split(coeffs[None], lax.axis...  28.4 us
  transfers between devices with their start and end apart: 2, of which 2 were waited for; matrix products, arithmetic and copies ran while one was open for 1% of the time, Pallas kernels for 0%

profile of v1, /device:TPU:1, one launch (start us, length us, event | category | flops | bytes accessed | tf_op | source)
XLA Modules:
  0.0 601.6 jit_solution(7428835626858671512)
XLA Ops:
  0.7 18.3 %multiply_convert_fusion.1 = (bf16[8192,16,1,8]{0,3,2,1:T(8,128)(2,1)S(1)}, bf16[8192,16,1,8]{0,3,2,1:T(8,128)(2,1)S(1)}) fusion(s32[16,8]{1,0:T(8,128)S(1)} %mul.96), kind=kLoop, calls=%fused_computation.19 | loop fusion | flops 19922944 | bytes 4194816 | tf_op jit(solution)/shard_map/convert
  19.5 3.0 copy-done.3
  22.4 2.4 fusion.22
  25.9 1.7 reshape.240
  27.6 8.6 %all-to-all-start = ((bf16[16,2,4096]{2,1,0:T(2,128)(2,1)}), bf16[16,2,4096]{2,1,0:T(2,128)(2,1)S(1)}, u32[]{:S(2)}, u32[]{:S(2)}) async-start(bf16[16,2,4096]{2,1,0:T(2,128)(2,1)} %reshape.240), calls=%async_computation | async-start | bytes 524288 | tf_op jit(solution)/shard_map/all_to_all | solution.py:91
  36.2 3.2 sort.17
  39.4 4.2 all-to-all-done
  45.3 1.4 slice.66
  46.7 1.4 slice.68
  48.2 1.4 slice.70
  49.6 3.6 slice.72
  53.2 3.5 slice.74
  56.7 1.4 slice.76
  58.1 1.4 slice.78
  59.6 1.4 slice.80
  61.1 2.1 convolution_convert_fusion.7
  64.3 2.1 convolution_convert_fusion.6
  67.4 2.9 convolution_convert_fusion.5
  70.3 2.5 stack.79
  72.8 1.7 copy.171
  75.8 2.9 convolution_convert_fusion.4
  78.7 3.7 stack.80
  82.3 1.6 copy.172
  84.0 1.4 reshape.216
  85.3 2.9 convolution_convert_fusion.3
  88.2 3.7 stack.81
  93.3 2.9 convolution_convert_fusion.2
  96.2 3.7 stack.82
  100.0 2.9 convolution_convert_fusion.1
  102.9 3.7 stack.83
  106.7 2.9 convolution_convert_fusion
  109.5 3.7 stack.84
  113.2 21.4 %stack.67 = bf16[1,32,2,8,4096]{4,3,2,1,0:T(8,128)(2,1)} concatenate(bf16[1,32,2,1,4096]{4,3,2,1,0:T(2,128)(2,1)S(1)} %stack.77, bf16[1,32,2,1,4096]{4,3,2,1,0:T(2,128)(2,1)S(1)} %stack.78, bf16[1,32,2,1,4096]{4,3,2,1,0:T(2,128)(2,1)S(1)} %stack.79, bf16[1,32,2,1,4096]{4,3,2,1,0:T(2,128)(2,1)} %stack.80, bf16[1,32,2,1,4096]{4,3,2,1,0:T(2,128)(2,1)} %stack.81, ...), dimensions={3} | concatenate | bytes 8388608 | tf_op jit(solution)/shard_map/stack | solution.py:98
  143.3 54.8 %all_to_all.41 = bf16[8,1,32,2,8,512]{5,4,3,2,1,0:T(8,128)(2,1)} all-to-all(bf16[8,1,32,2,8,512]{5,4,3,2,1,0:T(8,128)(2,1)S(1)} %fusion.23), channel_id=1, replica_groups=mesh['freq'=8,'blk'=16] {'freq'}, dimensions={0} | all-to-all | bytes 8388608 | tf_op jit(solution)/shard_map/all_to_all | solution.py:102
  198.1 28.4 %copy.184 = bf16[8,32,2,8,512]{1,3,2,0,4:T(8,128)(2,1)} copy(bf16[8,32,2,8,512]{4,3,2,1,0:T(8,128)(2,1)} %bitcast.134) | data formatting | bytes 8388608 | tf_op jit(solution)/shard_map/reshape | solution.py:101
  226.5 20.7 %reshape.242 = bf16[16,2,65536]{2,1,0:T(2,128)(2,1)} reshape(bf16[512,8,2,8,32]{4,3,2,1,0:T(8,128)(2,1)} %bitcast.132) | data formatting | bytes 8388608
  247.3 4.9 all-to-all-start.2
  252.8 62.7 %all-to-all-done.2 = bf16[16,2,65536]{2,1,0:T(2,128)(2,1)} async-done(((bf16[16,2,65536]{2,1,0:T(2,128)(2,1)}), bf16[16,2,65536]{2,1,0:T(2,128)(2,1)}, u32[]{:S(2)}, u32[]{:S(2)}) %all-to-all-start.2) | async-done | bytes 4194336 | tf_op jit(solution)/shard_map/all_to_all | solution.py:100
  315.4 16.0 %reshape.243 = bf16[512,8,2,8,32]{4,3,2,1,0:T(8,128)(2,1)} reshape(bf16[16,2,65536]{2,1,0:T(2,128)(2,1)} %all-to-all-done.2) | data formatting | bytes 8388608
  331.5 36.1 %copy.186 = bf16[8,32,2,16,8,32]{5,4,3,2,1,0:T(8,128)(2,1)} copy(bf16[8,32,2,16,8,32]{1,4,2,0,5,3:T(8,128)(2,1)} %bitcast.133) | data formatting | bytes 8388608 | tf_op jit(solution)/shard_map/all_to_all | solution.py:100
  367.6 14.3 %broadcast_multiply_fusion = bf16[8,32,2,128,32]{4,3,2,1,0:T(8,128)(2,1)} fusion(bf16[128]{0:T(256)(128)(2,1)S(1)} %fusion.43, bf16[8,32,2,16,8,32]{5,4,3,2,1,0:T(8,128)(2,1)} %copy.186), kind=kLoop, calls=%fused_computation.2 | loop fusion | flops 2097152 | bytes 8388864 | tf_op jit(solution)/shard_map/mul | solution.py:41
  381.9 16.1 %copy.188 = bf16[8,32,2,128,32]{3,0,1,2,4:T(8,128)(2,1)} copy(bf16[8,32,2,128,32]{4,3,2,1,0:T(8,128)(2,1)} %broadcast_multiply_fusion) | data formatting | bytes 8388608 | tf_op jit(solution)/shard_map/mul | solution.py:41
  397.9 16.0 %copy.187 = bf16[8,32,2,128,32]{3,0,1,2,4:T(8,128)(2,1)} copy(bf16[8,32,2,128,32]{4,3,2,1,0:T(8,128)(2,1)} %bitcast.131) | data formatting | bytes 8388608 | tf_op jit(solution)/shard_map/all_to_all | solution.py:100
  413.9 6.3 %convolution_bitcast_fusion = f32[8,8,32]{0,1,2:T(8,128)S(1)} fusion(bf16[8,32,2,128,32]{3,0,1,2,4:T(8,128)(2,1)} %copy.187, bf16[8,32,2,128,32]{3,0,1,2,4:T(8,128)(2,1)} %copy.188), kind=kOutput, calls=%fused_computation.41 | convolution fusion | flops 33554432 | bytes 8396800 | tf_op jit(solution)/shard_map/ikcsl,jkcsl->ijl/dot_general | solution.py:42
  420.5 67.2 %psum.7 = f32[128,64]{0,1:T(8,128)S(1)} all-reduce(f32[128,64]{0,1:T(8,128)S(1)} %fusion.31), channel_id=1, replica_groups=mesh['freq'=8,'blk'=16] {'freq','blk'}, use_global_device_ids=true, to_apply=%region_2.3 | all-reduce | flops 8192 | bytes 65536 | tf_op jit(solution)/shard_map/psum | solution.py:52
  488.2 93.9 %custom-call.11 = f32[128,8,8]{2,1,0:T(8,128)S(1)} custom-call(f32[128,8,8]{2,1,0:T(8,128)S(1)} %broadcast_multiply_fusion.1), custom_call_target="Cholesky" | custom-call | tf_op jit(solution)/shard_map/jit(cholesky)/cholesky | solution.py:24
  584.9 13.2 %multiply_reduce_fusion = f32[32,32,2,128]{0,3,2,1:T(8,128)} fusion(f32[32,8]{0,1:T(8,128)S(1)} %fusion.33, bf16[8,32,2,16,8,32]{5,4,3,2,1,0:T(8,128)(2,1)} %copy.186), kind=kLoop, calls=%fused_computation.1 | loop fusion | flops 6029312 | bytes 5243904
  598.0 3.6 copy.208
  (70 shorter events, 21.6 us)
Async XLA Ops:
  19.1 3.4 copy-start.3
  22.4 13.8 %copy-start = (s32[256]{0:T(256)S(1)}, s32[256]{0:T(256)}, u32[]{:S(2)}) copy-start(s32[256]{0:T(256)} %param.8) | copy-start | bytes 3076
  27.6 16.1 %all-to-all-start = ((bf16[16,2,4096]{2,1,0:T(2,128)(2,1)}), bf16[16,2,4096]{2,1,0:T(2,128)(2,1)S(1)}, u32[]{:S(2)}, u32[]{:S(2)}) async-start(bf16[16,2,4096]{2,1,0:T(2,128)(2,1)} %reshape.240), calls=%async_computation | async-start | bytes 524288 | tf_op jit(solution)/shard_map/all_to_all | solution.py:91
  247.3 4.9 copy-start.1
  247.3 5.4 copy-start.2
  247.3 68.1 %all-to-all-start.2 = ((bf16[16,2,65536]{2,1,0:T(2,128)(2,1)}), bf16[16,2,65536]{2,1,0:T(2,128)(2,1)}, u32[]{:S(2)}, u32[]{:S(2)}) async-start(bf16[16,2,65536]{2,1,0:T(2,128)(2,1)} %reshape.242), calls=%async_computation.2 | async-start | bytes 8388608 | tf_op jit(solution)/shard_map/all_to_all | solution.py:100
